TPU v7x, 256 devices: a whole 4x4x8 slice. The times are simulated.
256 devices in a mesh: dp: 64 (over z_lo, y, x, core), mp: 4 (over z_hi).
Axes of the slice: x: 4, y: 4, z: 8 (z_hi: 4, z_lo: 2; z = z_hi * 2 + z_lo), core: 2. Of those that a mesh axis runs over, the one named last changes fastest.
Arguments:
- pooled_rows: float32 [8192, 1152], P('dp', 'mp'), may hold values from -8 to 8
- projection: float32 [1152, 1152], P('mp'), may hold values from -0.1875 to 0.1875
- text_rows: float32 [8192, 1152], P(('dp', 'mp')), may hold values from -8 to 8
- caption_row: int32 [8192], P('dp'), may hold values from 0 to 8191, as said below
Outputs:
- pooled_grad: float32 [8192, 1152], P('dp', 'mp')
- text_grad: float32 [8192, 1152], P(('dp', 'mp'))
Inputs may be any that keep to these rules, and one draw needn't show every extreme that they name: `caption_row`: every caption row is named by exactly one image. Of the 128 images of one index of dp, those whose caption row lies in the block of 128 rows of any one index (its own included) number 1 to 3; 3 is reached by some pair of indices.
All inputs are finite; a program needn't handle non-finite values.
Results may differ from a plain program's by a relative error of at most 0.0003.
Values sent between devices are 32-bit elements; how exact they have to be, the bound alone decides.
No kernel may reach another device: no remote copies, remote signals or barrier semaphores. Data moves between devices by JAX's collectives and lax.ppermute only.
A program may use at most 64 MiB of HBM per device.

v0:
```python
import jax
import jax.numpy as jnp
from jax import lax
from jax.sharding import PartitionSpec as P

LOGIT_SCALE = 10.0
LOGIT_BIAS = -2.0
NORM_EPS = 1e-06


def shifted(value, axis, steps):
    count = lax.axis_size(axis)
    pairs = [(source, (source + steps) % count) for source in range(count)]
    return lax.ppermute(value, axis, pairs)


def product(left, right):
    return jnp.dot(left, right, precision=lax.Precision.HIGHEST, preferred_element_type=jnp.float32)


def product_nt(left, right):
    return lax.dot_general(
        left,
        right,
        (((1,), (1,)), ((), ())),
        precision=lax.Precision.HIGHEST,
        preferred_element_type=jnp.float32,
    )


def product_tn(left, right):
    return lax.dot_general(
        left,
        right,
        (((0,), (0,)), ((), ())),
        precision=lax.Precision.HIGHEST,
        preferred_element_type=jnp.float32,
    )


def unit_rows(raw):
    scale = lax.rsqrt(jnp.sum(raw * raw, axis=1) + NORM_EPS)
    return (raw * scale[:, None], scale)


def unit_back(unit, scale, grad):
    return scale[:, None] * (grad - unit * jnp.sum(unit * grad, axis=1, keepdims=True))


def pair_terms(images, captions, image_rows, caption_rows):
    logits = LOGIT_SCALE * product_nt(images, captions) + LOGIT_BIAS
    target = image_rows[:, None] == caption_rows[None, :]
    signs = jnp.where(target, 1.0, -1.0).astype(jnp.float32)
    weights = -signs * jax.nn.sigmoid(-signs * logits)
    return (LOGIT_SCALE * product(weights, captions), LOGIT_SCALE * product_tn(weights, images))


def local(pooled_rows, projection, text_rows, caption_row):
    shards = lax.axis_size("dp")
    own_index = lax.axis_index("dp")
    column = lax.axis_index("mp")
    per_shard = pooled_rows.shape[0]
    features = pooled_rows.shape[1]
    text_count = text_rows.shape[0]
    base = per_shard // shards
    capacity = base + min(3, base - 1)
    owner = caption_row // per_shard
    target_slot = caption_row % per_shard
    onehot = (owner[:, None] == jnp.arange(shards, dtype=jnp.int32)[None, :]).astype(jnp.int32)
    before = jnp.cumsum(onehot, axis=0) - onehot
    rank = jnp.sum(before * onehot, axis=1)
    position = owner * capacity + rank
    outgoing = jnp.zeros((shards * capacity, features), jnp.float32).at[position].set(pooled_rows)
    out_slots = jnp.full((shards * capacity,), per_shard, jnp.int32).at[position].set(target_slot)
    arrived, arrived_slots = (
        lax.all_to_all(outgoing, "dp", split_axis=0, concat_axis=0, tiled=True),
        lax.all_to_all(out_slots, "dp", split_axis=0, concat_axis=0, tiled=True),
    )
    arranged = (
        jnp.zeros((per_shard, features), jnp.float32).at[arrived_slots].set(arrived, mode="drop")
    )
    projected = lax.psum(product(arranged, projection), "mp")
    images, image_scale = unit_rows(projected)
    captions, caption_scale = unit_rows(text_rows)
    image_rows = own_index * per_shard + jnp.arange(per_shard, dtype=jnp.int32)
    local_rows = column * text_count + jnp.arange(text_count, dtype=jnp.int32)
    image_zero = jnp.zeros(images.shape, jnp.float32)

    def visit(anchor, image_grad, visiting, visit_grad):
        image_term, caption_term = pair_terms(
            images, visiting, image_rows, anchor * per_shard + local_rows
        )
        return (image_grad + image_term, visit_grad + caption_term)

    def tour_step(turn, carry):
        image_grad, visiting, visit_grad = carry
        anchor = (own_index - turn) % shards
        image_grad, visit_grad = visit(anchor, image_grad, visiting, visit_grad)
        visiting, visit_grad = shifted((visiting, visit_grad), "dp", 1)
        return (image_grad, visiting, visit_grad)

    initial = (image_zero, captions, jnp.zeros(captions.shape, jnp.float32))
    image_grad, visiting, visit_grad = lax.fori_loop(0, shards - 1, tour_step, initial)
    image_grad, visit_grad = visit((own_index + 1) % shards, image_grad, visiting, visit_grad)
    caption_grad = shifted(visit_grad, "dp", 1)
    image_grad = lax.psum(image_grad, "mp")
    raw_grad = unit_back(images, image_scale, image_grad)
    column_grad = product_nt(raw_grad, projection)
    returning = jnp.take(column_grad, arrived_slots, axis=0, mode="fill", fill_value=0.0)
    came_back = lax.all_to_all(returning, "dp", split_axis=0, concat_axis=0, tiled=True)
    pooled_grad = came_back[position]
    text_grad = unit_back(captions, caption_scale, caption_grad)
    return (pooled_grad, text_grad)


def solution(mesh):
    placed = (P("dp", "mp"), P("mp", None), P(("dp", "mp"), None), P("dp"))
    return jax.shard_map(
        local,
        mesh=mesh,
        in_specs=placed,
        out_specs=(P("dp", "mp"), P(("dp", "mp"), None)),
        check_vma=False,
    )
```

profile of v0, /device:TPU:1, one launch (start us, length us, event | category | flops | bytes accessed | tf_op | source)
XLA Modules:
  0.0 848.4 jit_solution(17598125918919216452)
XLA Ops:
  10.1 10.3 %all-to-all-start = ((s32[64,3,1]{1,2,0:T(1,128)}), s32[64,3,1]{1,2,0:T(1,128)S(1)}, u32[]{:S(2)}, u32[]{:S(2)}) async-start(s32[64,3,1]{1,2,0:T(1,128)} %bitcast), calls=%async_computation | async-start | bytes 65536 | tf_op jit(solution)/shard_map/all_to_all | solution.py:77
  34.9 9.4 %all-to-all-done.1 = f32[64,3,288]{2,1,0:T(4,128)S(1)} async-done(((f32[64,3,288]{2,1,0:T(4,128)}), f32[64,3,288]{2,1,0:T(4,128)S(1)}, u32[]{:S(2)}, u32[]{:S(2)}) %all-to-all-start.1) | async-done | bytes 221216 | tf_op jit(solution)/shard_map/all_to_all | solution.py:76
  48.7 52.0 %all-reduce.3.cloned.1.call-done = f32[128,1152]{1,0:T(8,128)} async-done(((f32[128,1152]{1,0:T(8,128)}), f32[128,1152]{1,0:T(8,128)}) %all-reduce.3.cloned.1.call-update) | async-done | bytes 589840 | tf_op jit(solution)/shard_map/psum | solution.py:82
  103.7 652.1 %while.20 = (s32[]{:T(128)}, f32[128,1152]{1,0:T(8,128)S(1)}, f32[32,1152]{1,0:T(8,128)S(1)}, f32[32,1152]{1,0:T(8,128)S(1)}, s32[]{:T(128)}, /*index=5*/f32[128...) while((s32[]{:T(128)}, f32[128,1152]{1,0:T(8,128)S(1)}, ...), condition=%wide.region_9.10_spmd.clone, body=%wide.region_8.9_spmd.clone.sunk | while | flops 170426576 | bytes 4474472 | solution.py:103
  171.9 8.3 collective-permute-done.1
  224.2 8.3 collective-permute-done.1
  245.2 8.3 collective-permute-done.1
  266.1 8.3 collective-permute-done.1
  339.3 8.3 collective-permute-done.1
  391.7 8.3 collective-permute-done.1
  412.6 8.3 collective-permute-done.1
  433.5 8.3 collective-permute-done.1
  464.9 8.3 collective-permute-done.1
  506.8 8.3 collective-permute-done.1
  559.1 8.3 collective-permute-done.1
  580.0 8.3 collective-permute-done.1
  600.9 8.3 collective-permute-done.1
  674.2 8.3 collective-permute-done.1
  726.5 8.3 collective-permute-done.1
  747.4 8.3 collective-permute-done.1
  758.8 9.0 %collective-permute-done.2 = f32[32,1152]{1,0:T(8,128)S(1)} collective-permute-done((f32[32,1152]{1,0:T(8,128)S(1)}, f32[32,1152]{1,0:T(8,128)S(1)}, u32[]{:S(2)}, u32[]{:S(2)}) %collective-permute-start.2) | collective-permute-done | bytes 147488 | tf_op jit(solution)/shard_map/ppermute | solution.py:14
  768.0 46.4 %all-reduce.5.cloned.1.call-done = f32[128,1152]{1,0:T(8,128)} async-done(((f32[128,1152]{1,0:T(8,128)}), f32[128,1152]{1,0:T(8,128)}) %all-reduce.5.cloned.1.call-update) | async-done | bytes 589840 | tf_op jit(solution)/shard_map/psum | solution.py:106
  819.4 9.4 %all-to-all-start.2 = ((f32[64,3,288]{2,1,0:T(4,128)}), f32[64,3,288]{2,1,0:T(4,128)S(1)}, u32[]{:S(2)}, u32[]{:S(2)}) async-start(f32[64,3,288]{2,1,0:T(4,128)} %broadcast_select_fusion), calls=%async_computation.2 | async-start | bytes 786432 | tf_op jit(solution)/shard_map/all_to_all | solution.py:110
  829.6 10.1 %all-to-all-done.2 = f32[64,3,288]{2,1,0:T(4,128)S(1)} async-done(((f32[64,3,288]{2,1,0:T(4,128)}), f32[64,3,288]{2,1,0:T(4,128)S(1)}, u32[]{:S(2)}, u32[]{:S(2)}) %all-to-all-start.2) | async-done | bytes 221216 | tf_op jit(solution)/shard_map/all_to_all | solution.py:110
  (692 shorter events, 549.4 us)
Async XLA Ops:
  10.1 18.1 %all-to-all-start = ((s32[64,3,1]{1,2,0:T(1,128)}), s32[64,3,1]{1,2,0:T(1,128)S(1)}, u32[]{:S(2)}, u32[]{:S(2)}) async-start(s32[64,3,1]{1,2,0:T(1,128)} %bitcast), calls=%async_computation | async-start | bytes 65536 | tf_op jit(solution)/shard_map/all_to_all | solution.py:77
  28.3 16.1 %all-to-all-start.1 = ((f32[64,3,288]{2,1,0:T(4,128)}), f32[64,3,288]{2,1,0:T(4,128)S(1)}, u32[]{:S(2)}, u32[]{:S(2)}) async-start(f32[64,3,288]{2,1,0:T(4,128)} %all_to_all.28), calls=%async_computation.1 | async-start | bytes 786432 | tf_op jit(solution)/shard_map/all_to_all | solution.py:76
  33.5 67.2 %all-reduce.3.cloned.1.call-start = ((), (), s32[]{:S(2)}) async-start(), calls=%async_computation.3 | async-start | bytes 1179648 | tf_op jit(solution)/shard_map/psum | solution.py:82
  47.9 766.5 %all-reduce.5.cloned.1.call-start = ((), (), s32[]{:S(2)}) async-start(), calls=%async_computation.4 | async-start | bytes 1179648 | tf_op jit(solution)/shard_map/psum | solution.py:106
  127.9 10.4 %collective-permute-start = (f32[32,1152]{1,0:T(8,128)S(1)}, f32[32,1152]{1,0:T(8,128)S(1)}, u32[]{:S(2)}, u32[]{:S(2)}) collective-permute-start(f32[32,1152]{1,0:T(8,128)S(1)} %copy.23), channel_id=1, source_target_pairs={{0,4},{4,8},{8,12},{12,16},{16,20},{20,24},{24,28},{28,32},{32,36}... | collective-permute-start | bytes 442376 | tf_op jit(solution)/shard_map/while/body/eval_jaxpr/ppermute | solution.py:14
  169.8 10.4 %collective-permute-start = (f32[32,1152]{1,0:T(8,128)S(1)}, f32[32,1152]{1,0:T(8,128)S(1)}, u32[]{:S(2)}, u32[]{:S(2)}) collective-permute-start(f32[32,1152]{1,0:T(8,128)S(1)} %copy.23), channel_id=1, source_target_pairs={{0,4},{4,8},{8,12},{12,16},{16,20},{20,24},{24,28},{28,32},{32,36}... | collective-permute-start | bytes 442376 | tf_op jit(solution)/shard_map/while/body/eval_jaxpr/ppermute | solution.py:14
  190.7 10.4 %collective-permute-start = (f32[32,1152]{1,0:T(8,128)S(1)}, f32[32,1152]{1,0:T(8,128)S(1)}, u32[]{:S(2)}, u32[]{:S(2)}) collective-permute-start(f32[32,1152]{1,0:T(8,128)S(1)} %copy.23), channel_id=1, source_target_pairs={{0,4},{4,8},{8,12},{12,16},{16,20},{20,24},{24,28},{28,32},{32,36}... | collective-permute-start | bytes 442376 | tf_op jit(solution)/shard_map/while/body/eval_jaxpr/ppermute | solution.py:14
  211.6 10.4 %collective-permute-start = (f32[32,1152]{1,0:T(8,128)S(1)}, f32[32,1152]{1,0:T(8,128)S(1)}, u32[]{:S(2)}, u32[]{:S(2)}) collective-permute-start(f32[32,1152]{1,0:T(8,128)S(1)} %copy.23), channel_id=1, source_target_pairs={{0,4},{4,8},{8,12},{12,16},{16,20},{20,24},{24,28},{28,32},{32,36}... | collective-permute-start | bytes 442376 | tf_op jit(solution)/shard_map/while/body/eval_jaxpr/ppermute | solution.py:14
  222.1 10.4 %collective-permute-start = (f32[32,1152]{1,0:T(8,128)S(1)}, f32[32,1152]{1,0:T(8,128)S(1)}, u32[]{:S(2)}, u32[]{:S(2)}) collective-permute-start(f32[32,1152]{1,0:T(8,128)S(1)} %copy.23), channel_id=1, source_target_pairs={{0,4},{4,8},{8,12},{12,16},{16,20},{20,24},{24,28},{28,32},{32,36}... | collective-permute-start | bytes 442376 | tf_op jit(solution)/shard_map/while/body/eval_jaxpr/ppermute | solution.py:14
  243.0 10.4 %collective-permute-start = (f32[32,1152]{1,0:T(8,128)S(1)}, f32[32,1152]{1,0:T(8,128)S(1)}, u32[]{:S(2)}, u32[]{:S(2)}) collective-permute-start(f32[32,1152]{1,0:T(8,128)S(1)} %copy.23), channel_id=1, source_target_pairs={{0,4},{4,8},{8,12},{12,16},{16,20},{20,24},{24,28},{28,32},{32,36}... | collective-permute-start | bytes 442376 | tf_op jit(solution)/shard_map/while/body/eval_jaxpr/ppermute | solution.py:14
  263.9 10.4 %collective-permute-start = (f32[32,1152]{1,0:T(8,128)S(1)}, f32[32,1152]{1,0:T(8,128)S(1)}, u32[]{:S(2)}, u32[]{:S(2)}) collective-permute-start(f32[32,1152]{1,0:T(8,128)S(1)} %copy.23), channel_id=1, source_target_pairs={{0,4},{4,8},{8,12},{12,16},{16,20},{20,24},{24,28},{28,32},{32,36}... | collective-permute-start | bytes 442376 | tf_op jit(solution)/shard_map/while/body/eval_jaxpr/ppermute | solution.py:14
  295.3 10.4 %collective-permute-start = (f32[32,1152]{1,0:T(8,128)S(1)}, f32[32,1152]{1,0:T(8,128)S(1)}, u32[]{:S(2)}, u32[]{:S(2)}) collective-permute-start(f32[32,1152]{1,0:T(8,128)S(1)} %copy.23), channel_id=1, source_target_pairs={{0,4},{4,8},{8,12},{12,16},{16,20},{20,24},{24,28},{28,32},{32,36}... | collective-permute-start | bytes 442376 | tf_op jit(solution)/shard_map/while/body/eval_jaxpr/ppermute | solution.py:14
  337.2 10.4 %collective-permute-start = (f32[32,1152]{1,0:T(8,128)S(1)}, f32[32,1152]{1,0:T(8,128)S(1)}, u32[]{:S(2)}, u32[]{:S(2)}) collective-permute-start(f32[32,1152]{1,0:T(8,128)S(1)} %copy.23), channel_id=1, source_target_pairs={{0,4},{4,8},{8,12},{12,16},{16,20},{20,24},{24,28},{28,32},{32,36}... | collective-permute-start | bytes 442376 | tf_op jit(solution)/shard_map/while/body/eval_jaxpr/ppermute | solution.py:14
  358.1 10.4 %collective-permute-start = (f32[32,1152]{1,0:T(8,128)S(1)}, f32[32,1152]{1,0:T(8,128)S(1)}, u32[]{:S(2)}, u32[]{:S(2)}) collective-permute-start(f32[32,1152]{1,0:T(8,128)S(1)} %copy.23), channel_id=1, source_target_pairs={{0,4},{4,8},{8,12},{12,16},{16,20},{20,24},{24,28},{28,32},{32,36}... | collective-permute-start | bytes 442376 | tf_op jit(solution)/shard_map/while/body/eval_jaxpr/ppermute | solution.py:14
  379.0 10.4 %collective-permute-start = (f32[32,1152]{1,0:T(8,128)S(1)}, f32[32,1152]{1,0:T(8,128)S(1)}, u32[]{:S(2)}, u32[]{:S(2)}) collective-permute-start(f32[32,1152]{1,0:T(8,128)S(1)} %copy.23), channel_id=1, source_target_pairs={{0,4},{4,8},{8,12},{12,16},{16,20},{20,24},{24,28},{28,32},{32,36}... | collective-permute-start | bytes 442376 | tf_op jit(solution)/shard_map/while/body/eval_jaxpr/ppermute | solution.py:14
  389.5 10.4 %collective-permute-start = (f32[32,1152]{1,0:T(8,128)S(1)}, f32[32,1152]{1,0:T(8,128)S(1)}, u32[]{:S(2)}, u32[]{:S(2)}) collective-permute-start(f32[32,1152]{1,0:T(8,128)S(1)} %copy.23), channel_id=1, source_target_pairs={{0,4},{4,8},{8,12},{12,16},{16,20},{20,24},{24,28},{28,32},{32,36}... | collective-permute-start | bytes 442376 | tf_op jit(solution)/shard_map/while/body/eval_jaxpr/ppermute | solution.py:14
  410.4 10.4 %collective-permute-start = (f32[32,1152]{1,0:T(8,128)S(1)}, f32[32,1152]{1,0:T(8,128)S(1)}, u32[]{:S(2)}, u32[]{:S(2)}) collective-permute-start(f32[32,1152]{1,0:T(8,128)S(1)} %copy.23), channel_id=1, source_target_pairs={{0,4},{4,8},{8,12},{12,16},{16,20},{20,24},{24,28},{28,32},{32,36}... | collective-permute-start | bytes 442376 | tf_op jit(solution)/shard_map/while/body/eval_jaxpr/ppermute | solution.py:14
  431.4 10.4 %collective-permute-start = (f32[32,1152]{1,0:T(8,128)S(1)}, f32[32,1152]{1,0:T(8,128)S(1)}, u32[]{:S(2)}, u32[]{:S(2)}) collective-permute-start(f32[32,1152]{1,0:T(8,128)S(1)} %copy.23), channel_id=1, source_target_pairs={{0,4},{4,8},{8,12},{12,16},{16,20},{20,24},{24,28},{28,32},{32,36}... | collective-permute-start | bytes 442376 | tf_op jit(solution)/shard_map/while/body/eval_jaxpr/ppermute | solution.py:14
  462.8 10.4 %collective-permute-start = (f32[32,1152]{1,0:T(8,128)S(1)}, f32[32,1152]{1,0:T(8,128)S(1)}, u32[]{:S(2)}, u32[]{:S(2)}) collective-permute-start(f32[32,1152]{1,0:T(8,128)S(1)} %copy.23), channel_id=1, source_target_pairs={{0,4},{4,8},{8,12},{12,16},{16,20},{20,24},{24,28},{28,32},{32,36}... | collective-permute-start | bytes 442376 | tf_op jit(solution)/shard_map/while/body/eval_jaxpr/ppermute | solution.py:14
  504.6 10.4 %collective-permute-start = (f32[32,1152]{1,0:T(8,128)S(1)}, f32[32,1152]{1,0:T(8,128)S(1)}, u32[]{:S(2)}, u32[]{:S(2)}) collective-permute-start(f32[32,1152]{1,0:T(8,128)S(1)} %copy.23), channel_id=1, source_target_pairs={{0,4},{4,8},{8,12},{12,16},{16,20},{20,24},{24,28},{28,32},{32,36}... | collective-permute-start | bytes 442376 | tf_op jit(solution)/shard_map/while/body/eval_jaxpr/ppermute | solution.py:14
  577.9 10.4 %collective-permute-start = (f32[32,1152]{1,0:T(8,128)S(1)}, f32[32,1152]{1,0:T(8,128)S(1)}, u32[]{:S(2)}, u32[]{:S(2)}) collective-permute-start(f32[32,1152]{1,0:T(8,128)S(1)} %copy.23), channel_id=1, source_target_pairs={{0,4},{4,8},{8,12},{12,16},{16,20},{20,24},{24,28},{28,32},{32,36}... | collective-permute-start | bytes 442376 | tf_op jit(solution)/shard_map/while/body/eval_jaxpr/ppermute | solution.py:14
  598.8 10.4 %collective-permute-start = (f32[32,1152]{1,0:T(8,128)S(1)}, f32[32,1152]{1,0:T(8,128)S(1)}, u32[]{:S(2)}, u32[]{:S(2)}) collective-permute-start(f32[32,1152]{1,0:T(8,128)S(1)} %copy.23), channel_id=1, source_target_pairs={{0,4},{4,8},{8,12},{12,16},{16,20},{20,24},{24,28},{28,32},{32,36}... | collective-permute-start | bytes 442376 | tf_op jit(solution)/shard_map/while/body/eval_jaxpr/ppermute | solution.py:14
  745.3 10.4 %collective-permute-start = (f32[32,1152]{1,0:T(8,128)S(1)}, f32[32,1152]{1,0:T(8,128)S(1)}, u32[]{:S(2)}, u32[]{:S(2)}) collective-permute-start(f32[32,1152]{1,0:T(8,128)S(1)} %copy.23), channel_id=1, source_target_pairs={{0,4},{4,8},{8,12},{12,16},{16,20},{20,24},{24,28},{28,32},{32,36}... | collective-permute-start | bytes 442376 | tf_op jit(solution)/shard_map/while/body/eval_jaxpr/ppermute | solution.py:14
  819.4 20.3 %all-to-all-start.2 = ((f32[64,3,288]{2,1,0:T(4,128)}), f32[64,3,288]{2,1,0:T(4,128)S(1)}, u32[]{:S(2)}, u32[]{:S(2)}) async-start(f32[64,3,288]{2,1,0:T(4,128)} %broadcast_select_fusion), calls=%async_computation.2 | async-start | bytes 786432 | tf_op jit(solution)/shard_map/all_to_all | solution.py:110
  (122 other events, 1301.1 us)
Sparse Core Ops, SparseCore 0:
  48.0 52.5 all-reduce.2
  758.1 56.2 all-reduce.4
where the time goes:
time: 849 us; the launch traced here: 848 us
  waiting for transfers between devices  641 us (76%)
  matrix products  126 us (15%)
  starting transfers between devices  41.3 us (5%)
  between operations  14.4 us (2%)
  local copies, waits for them, and re-layouts  10.9 us (1%)
  other arithmetic  9.73 us (1%)
    ppermute x127, waiting for transfers between devices, shifted(): return lax.ppermute(value, axis, pairs)  519 us
    dot_general x65, matrix products, product(): jnp.dot(left, right, precision=lax.Precision.HIGHEST, preferred_element_t...  52.2 us
    psum x1, waiting for transfers between devices, local(): projected = lax.psum(product(arranged, projection), 'mp')  52 us
    psum x1, waiting for transfers between devices, local(): image_grad = lax.psum(image_grad, 'mp')  46.4 us
    dot_general x65, matrix products, product_nt(): lax.dot_general(left, right, (((1,), (1,)), ((), ())), precision=lax.Prec...  46.4 us
    dot_general x64, matrix products, product_tn(): lax.dot_general(left, right, (((0,), (0,)), ((), ())), precision=lax.Prec...  27.3 us
  transfers between devices with their start and end apart: 132, of which 69 were waited for; matrix products, arithmetic and copies ran while one was open for 15% of the time, Pallas kernels for 0%

commit v1 on v0

--- a/solution.py
+++ b/solution.py
@@ -79,7 +79,7 @@
     arranged = (
         jnp.zeros((per_shard, features), jnp.float32).at[arrived_slots].set(arrived, mode="drop")
     )
-    projected = lax.psum(product(arranged, projection), "mp")
+    projected = lax.all_gather(product(arranged, projection), "mp").sum(axis=0)
     images, image_scale = unit_rows(projected)
     captions, caption_scale = unit_rows(text_rows)
     image_rows = own_index * per_shard + jnp.arange(per_shard, dtype=jnp.int32)

time: 849 us -> 953 us (1.12)
  matrix products: 126 us -> 209 us
  other arithmetic: 9.73 us -> 41.8 us
    psum x1 -> x0, waiting for transfers between devices: 52 us -> none  [local(): projected = lax.psum(product(arranged, projection), 'mp')]
    all_gather x0 -> x1, waiting for transfers between devices: none -> 51.8 us  [local(): projected = lax.all_gather(product(arranged, projection), 'mp').sum(axis=0)]
    dot_general x64, matrix products: 27.3 us -> 69.1 us  [product_tn(): lax.dot_general(left, right, (((0,), (0,)), ((), ())), precision=lax.Prec...]
    dot_general x65, matrix products: 46.4 us -> 88.2 us  [product_nt(): lax.dot_general(left, right, (((1,), (1,)), ((), ())), precision=lax.Prec...]
    add x64, other arithmetic: 0.23 us -> 32.9 us  [local(): image_rows = own_index * per_shard + jnp.arange(per_shard, dtype=jnp.int32)]
  transfers between devices with their start and end apart: 132 -> 132, of which waited for: 69 -> 69; matrix products, arithmetic and copies ran while one was open for 15% -> 25% of each run, Pallas kernels for 0% -> 0%
where the time goes in v1:
time: 953 us; the launch traced here: 951 us
  waiting for transfers between devices  636 us (67%)
  matrix products  209 us (22%)
  other arithmetic  41.8 us (4%)
  starting transfers between devices  34.8 us (4%)
  between operations  14.3 us (2%)
  local copies, waits for them, and re-layouts  11.9 us (1%)
    ppermute x127, waiting for transfers between devices, shifted(): return lax.ppermute(value, axis, pairs)  515 us
    dot_general x65, matrix products, product_nt(): lax.dot_general(left, right, (((1,), (1,)), ((), ())), precision=lax.Prec...  88.2 us
    dot_general x64, matrix products, product_tn(): lax.dot_general(left, right, (((0,), (0,)), ((), ())), precision=lax.Prec...  69.1 us
    dot_general x65, matrix products, product(): jnp.dot(left, right, precision=lax.Precision.HIGHEST, preferred_element_t...  52.2 us
    all_gather x1, waiting for transfers between devices, local(): projected = lax.all_gather(product(arranged, projection), 'mp').sum(axis=0)  51.8 us
    psum x1, waiting for transfers between devices, local(): image_grad = lax.psum(image_grad, 'mp')  45.3 us
    add x64, other arithmetic, local(): image_rows = own_index * per_shard + jnp.arange(per_shard, dtype=jnp.int32)  32.9 us
  transfers between devices with their start and end apart: 132, of which 69 were waited for; matrix products, arithmetic and copies ran while one was open for 25% of the time, Pallas kernels for 0%

profile of v1, /device:TPU:1, one launch (start us, length us, event | category | flops | bytes accessed | tf_op | source)
XLA Modules:
  0.0 951.4 jit_solution(5633071794038677067)
XLA Ops:
  10.1 10.3 %all-to-all-start = ((s32[64,3,1]{1,2,0:T(1,128)}), s32[64,3,1]{1,2,0:T(1,128)S(1)}, u32[]{:S(2)}, u32[]{:S(2)}) async-start(s32[64,3,1]{1,2,0:T(1,128)} %bitcast), calls=%async_computation | async-start | bytes 65536 | tf_op jit(solution)/shard_map/all_to_all | solution.py:77
  34.4 9.6 %all-to-all-done.1 = f32[64,3,288]{2,1,0:T(4,128)S(1)} async-done(((f32[64,3,288]{2,1,0:T(4,128)}), f32[64,3,288]{2,1,0:T(4,128)S(1)}, u32[]{:S(2)}, u32[]{:S(2)}) %all-to-all-start.1) | async-done | bytes 221216 | tf_op jit(solution)/shard_map/all_to_all | solution.py:76
  50.1 51.8 %all-gather.3.cloned.1.call-done = f32[512,1152]{1,0:T(8,128)} async-done(((f32[128,1152]{1,0:T(8,128)}), f32[512,1152]{1,0:T(8,128)}) %all-gather.3.cloned.1.call-update) | async-done | bytes 2359312 | tf_op jit(solution)/shard_map/all_gather | solution.py:82
  104.5 754.6 %while.20 = (s32[]{:T(128)}, f32[128,1152]{1,0:T(8,128)S(1)}, f32[32,1152]{1,0:T(8,128)S(1)}, f32[32,1152]{1,0:T(8,128)S(1)}, s32[]{:T(128)}, /*index=5*/f32[128...) while((s32[]{:T(128)}, f32[128,1152]{1,0:T(8,128)S(1)}, ...), condition=%wide.region_9.10_spmd.clone, body=%wide.region_8.9_spmd.clone.sunk | while | flops 170426576 | bytes 4474472 | solution.py:103
  137.5 8.2 collective-permute-done.1
  161.6 8.2 collective-permute-done.1
  173.7 8.2 collective-permute-done.1
  185.8 8.2 collective-permute-done.1
  197.9 8.2 collective-permute-done.1
  210.0 8.2 collective-permute-done.1
  222.1 8.2 collective-permute-done.1
  246.3 8.2 collective-permute-done.1
  330.9 8.2 collective-permute-done.1
  391.4 8.2 collective-permute-done.1
  476.1 8.2 collective-permute-done.1
  560.7 8.2 collective-permute-done.1
  621.2 8.2 collective-permute-done.1
  705.8 8.2 collective-permute-done.1
  790.5 8.2 collective-permute-done.1
  850.9 8.2 collective-permute-done.1
  862.8 8.7 collective-permute-done.2
  872.2 45.3 %all-reduce.2.cloned.1.call-done = f32[128,1152]{1,0:T(8,128)} async-done(((f32[128,1152]{1,0:T(8,128)}), f32[128,1152]{1,0:T(8,128)}) %all-reduce.2.cloned.1.call-update) | async-done | bytes 589840 | tf_op jit(solution)/shard_map/psum | solution.py:106
  922.5 9.4 all-to-all-start.2
  932.6 10.1 %all-to-all-done.2 = f32[64,3,288]{2,1,0:T(4,128)S(1)} async-done(((f32[64,3,288]{2,1,0:T(4,128)}), f32[64,3,288]{2,1,0:T(4,128)S(1)}, u32[]{:S(2)}, u32[]{:S(2)}) %all-to-all-start.2) | async-done | bytes 221216 | tf_op jit(solution)/shard_map/all_to_all | solution.py:110
  (693 shorter events, 657.5 us)
Async XLA Ops:
  10.1 18.1 %all-to-all-start = ((s32[64,3,1]{1,2,0:T(1,128)}), s32[64,3,1]{1,2,0:T(1,128)S(1)}, u32[]{:S(2)}, u32[]{:S(2)}) async-start(s32[64,3,1]{1,2,0:T(1,128)} %bitcast), calls=%async_computation | async-start | bytes 65536 | tf_op jit(solution)/shard_map/all_to_all | solution.py:77
  28.3 15.7 %all-to-all-start.1 = ((f32[64,3,288]{2,1,0:T(4,128)}), f32[64,3,288]{2,1,0:T(4,128)S(1)}, u32[]{:S(2)}, u32[]{:S(2)}) async-start(f32[64,3,288]{2,1,0:T(4,128)} %all_to_all.28), calls=%async_computation.1 | async-start | bytes 786432 | tf_op jit(solution)/shard_map/all_to_all | solution.py:76
  33.0 68.9 %all-gather.3.cloned.1.call-start = ((), (), s32[]{:S(2)}) async-start(), calls=%async_computation.4 | async-start | bytes 2949120 | tf_op jit(solution)/shard_map/all_gather | solution.py:82
  47.6 869.9 %all-reduce.2.cloned.1.call-start = ((), (), s32[]{:S(2)}) async-start(), calls=%async_computation.3 | async-start | bytes 1179648 | tf_op jit(solution)/shard_map/psum | solution.py:106
  121.5 12.1 %collective-permute-start = (f32[32,1152]{1,0:T(8,128)S(1)}, f32[32,1152]{1,0:T(8,128)S(1)}, u32[]{:S(2)}, u32[]{:S(2)}) collective-permute-start(f32[32,1152]{1,0:T(8,128)S(1)} %copy.22), channel_id=1, source_target_pairs={{0,4},{4,8},{8,12},{12,16},{16,20},{20,24},{24,28},{28,32},{32,36}... | collective-permute-start | bytes 442376 | tf_op jit(solution)/shard_map/while/body/eval_jaxpr/ppermute | solution.py:14
  133.6 12.1 %collective-permute-start = (f32[32,1152]{1,0:T(8,128)S(1)}, f32[32,1152]{1,0:T(8,128)S(1)}, u32[]{:S(2)}, u32[]{:S(2)}) collective-permute-start(f32[32,1152]{1,0:T(8,128)S(1)} %copy.22), channel_id=1, source_target_pairs={{0,4},{4,8},{8,12},{12,16},{16,20},{20,24},{24,28},{28,32},{32,36}... | collective-permute-start | bytes 442376 | tf_op jit(solution)/shard_map/while/body/eval_jaxpr/ppermute | solution.py:14
  145.7 12.1 %collective-permute-start = (f32[32,1152]{1,0:T(8,128)S(1)}, f32[32,1152]{1,0:T(8,128)S(1)}, u32[]{:S(2)}, u32[]{:S(2)}) collective-permute-start(f32[32,1152]{1,0:T(8,128)S(1)} %copy.22), channel_id=1, source_target_pairs={{0,4},{4,8},{8,12},{12,16},{16,20},{20,24},{24,28},{28,32},{32,36}... | collective-permute-start | bytes 442376 | tf_op jit(solution)/shard_map/while/body/eval_jaxpr/ppermute | solution.py:14
  157.8 12.1 %collective-permute-start = (f32[32,1152]{1,0:T(8,128)S(1)}, f32[32,1152]{1,0:T(8,128)S(1)}, u32[]{:S(2)}, u32[]{:S(2)}) collective-permute-start(f32[32,1152]{1,0:T(8,128)S(1)} %copy.22), channel_id=1, source_target_pairs={{0,4},{4,8},{8,12},{12,16},{16,20},{20,24},{24,28},{28,32},{32,36}... | collective-permute-start | bytes 442376 | tf_op jit(solution)/shard_map/while/body/eval_jaxpr/ppermute | solution.py:14
  169.9 12.1 %collective-permute-start = (f32[32,1152]{1,0:T(8,128)S(1)}, f32[32,1152]{1,0:T(8,128)S(1)}, u32[]{:S(2)}, u32[]{:S(2)}) collective-permute-start(f32[32,1152]{1,0:T(8,128)S(1)} %copy.22), channel_id=1, source_target_pairs={{0,4},{4,8},{8,12},{12,16},{16,20},{20,24},{24,28},{28,32},{32,36}... | collective-permute-start | bytes 442376 | tf_op jit(solution)/shard_map/while/body/eval_jaxpr/ppermute | solution.py:14
  182.0 12.1 %collective-permute-start = (f32[32,1152]{1,0:T(8,128)S(1)}, f32[32,1152]{1,0:T(8,128)S(1)}, u32[]{:S(2)}, u32[]{:S(2)}) collective-permute-start(f32[32,1152]{1,0:T(8,128)S(1)} %copy.22), channel_id=1, source_target_pairs={{0,4},{4,8},{8,12},{12,16},{16,20},{20,24},{24,28},{28,32},{32,36}... | collective-permute-start | bytes 442376 | tf_op jit(solution)/shard_map/while/body/eval_jaxpr/ppermute | solution.py:14
  194.1 12.1 %collective-permute-start = (f32[32,1152]{1,0:T(8,128)S(1)}, f32[32,1152]{1,0:T(8,128)S(1)}, u32[]{:S(2)}, u32[]{:S(2)}) collective-permute-start(f32[32,1152]{1,0:T(8,128)S(1)} %copy.22), channel_id=1, source_target_pairs={{0,4},{4,8},{8,12},{12,16},{16,20},{20,24},{24,28},{28,32},{32,36}... | collective-permute-start | bytes 442376 | tf_op jit(solution)/shard_map/while/body/eval_jaxpr/ppermute | solution.py:14
  206.2 12.1 %collective-permute-start = (f32[32,1152]{1,0:T(8,128)S(1)}, f32[32,1152]{1,0:T(8,128)S(1)}, u32[]{:S(2)}, u32[]{:S(2)}) collective-permute-start(f32[32,1152]{1,0:T(8,128)S(1)} %copy.22), channel_id=1, source_target_pairs={{0,4},{4,8},{8,12},{12,16},{16,20},{20,24},{24,28},{28,32},{32,36}... | collective-permute-start | bytes 442376 | tf_op jit(solution)/shard_map/while/body/eval_jaxpr/ppermute | solution.py:14
  218.3 12.1 %collective-permute-start = (f32[32,1152]{1,0:T(8,128)S(1)}, f32[32,1152]{1,0:T(8,128)S(1)}, u32[]{:S(2)}, u32[]{:S(2)}) collective-permute-start(f32[32,1152]{1,0:T(8,128)S(1)} %copy.22), channel_id=1, source_target_pairs={{0,4},{4,8},{8,12},{12,16},{16,20},{20,24},{24,28},{28,32},{32,36}... | collective-permute-start | bytes 442376 | tf_op jit(solution)/shard_map/while/body/eval_jaxpr/ppermute | solution.py:14
  230.3 12.1 %collective-permute-start = (f32[32,1152]{1,0:T(8,128)S(1)}, f32[32,1152]{1,0:T(8,128)S(1)}, u32[]{:S(2)}, u32[]{:S(2)}) collective-permute-start(f32[32,1152]{1,0:T(8,128)S(1)} %copy.22), channel_id=1, source_target_pairs={{0,4},{4,8},{8,12},{12,16},{16,20},{20,24},{24,28},{28,32},{32,36}... | collective-permute-start | bytes 442376 | tf_op jit(solution)/shard_map/while/body/eval_jaxpr/ppermute | solution.py:14
  242.4 12.1 %collective-permute-start = (f32[32,1152]{1,0:T(8,128)S(1)}, f32[32,1152]{1,0:T(8,128)S(1)}, u32[]{:S(2)}, u32[]{:S(2)}) collective-permute-start(f32[32,1152]{1,0:T(8,128)S(1)} %copy.22), channel_id=1, source_target_pairs={{0,4},{4,8},{8,12},{12,16},{16,20},{20,24},{24,28},{28,32},{32,36}... | collective-permute-start | bytes 442376 | tf_op jit(solution)/shard_map/while/body/eval_jaxpr/ppermute | solution.py:14
  254.5 12.1 %collective-permute-start = (f32[32,1152]{1,0:T(8,128)S(1)}, f32[32,1152]{1,0:T(8,128)S(1)}, u32[]{:S(2)}, u32[]{:S(2)}) collective-permute-start(f32[32,1152]{1,0:T(8,128)S(1)} %copy.22), channel_id=1, source_target_pairs={{0,4},{4,8},{8,12},{12,16},{16,20},{20,24},{24,28},{28,32},{32,36}... | collective-permute-start | bytes 442376 | tf_op jit(solution)/shard_map/while/body/eval_jaxpr/ppermute | solution.py:14
  266.6 12.1 %collective-permute-start = (f32[32,1152]{1,0:T(8,128)S(1)}, f32[32,1152]{1,0:T(8,128)S(1)}, u32[]{:S(2)}, u32[]{:S(2)}) collective-permute-start(f32[32,1152]{1,0:T(8,128)S(1)} %copy.22), channel_id=1, source_target_pairs={{0,4},{4,8},{8,12},{12,16},{16,20},{20,24},{24,28},{28,32},{32,36}... | collective-permute-start | bytes 442376 | tf_op jit(solution)/shard_map/while/body/eval_jaxpr/ppermute | solution.py:14
  278.7 12.1 %collective-permute-start = (f32[32,1152]{1,0:T(8,128)S(1)}, f32[32,1152]{1,0:T(8,128)S(1)}, u32[]{:S(2)}, u32[]{:S(2)}) collective-permute-start(f32[32,1152]{1,0:T(8,128)S(1)} %copy.22), channel_id=1, source_target_pairs={{0,4},{4,8},{8,12},{12,16},{16,20},{20,24},{24,28},{28,32},{32,36}... | collective-permute-start | bytes 442376 | tf_op jit(solution)/shard_map/while/body/eval_jaxpr/ppermute | solution.py:14
  327.1 12.1 %collective-permute-start = (f32[32,1152]{1,0:T(8,128)S(1)}, f32[32,1152]{1,0:T(8,128)S(1)}, u32[]{:S(2)}, u32[]{:S(2)}) collective-permute-start(f32[32,1152]{1,0:T(8,128)S(1)} %copy.22), channel_id=1, source_target_pairs={{0,4},{4,8},{8,12},{12,16},{16,20},{20,24},{24,28},{28,32},{32,36}... | collective-permute-start | bytes 442376 | tf_op jit(solution)/shard_map/while/body/eval_jaxpr/ppermute | solution.py:14
  411.7 12.1 %collective-permute-start = (f32[32,1152]{1,0:T(8,128)S(1)}, f32[32,1152]{1,0:T(8,128)S(1)}, u32[]{:S(2)}, u32[]{:S(2)}) collective-permute-start(f32[32,1152]{1,0:T(8,128)S(1)} %copy.22), channel_id=1, source_target_pairs={{0,4},{4,8},{8,12},{12,16},{16,20},{20,24},{24,28},{28,32},{32,36}... | collective-permute-start | bytes 442376 | tf_op jit(solution)/shard_map/while/body/eval_jaxpr/ppermute | solution.py:14
  556.8 12.1 %collective-permute-start = (f32[32,1152]{1,0:T(8,128)S(1)}, f32[32,1152]{1,0:T(8,128)S(1)}, u32[]{:S(2)}, u32[]{:S(2)}) collective-permute-start(f32[32,1152]{1,0:T(8,128)S(1)} %copy.22), channel_id=1, source_target_pairs={{0,4},{4,8},{8,12},{12,16},{16,20},{20,24},{24,28},{28,32},{32,36}... | collective-permute-start | bytes 442376 | tf_op jit(solution)/shard_map/while/body/eval_jaxpr/ppermute | solution.py:14
  641.5 12.1 %collective-permute-start = (f32[32,1152]{1,0:T(8,128)S(1)}, f32[32,1152]{1,0:T(8,128)S(1)}, u32[]{:S(2)}, u32[]{:S(2)}) collective-permute-start(f32[32,1152]{1,0:T(8,128)S(1)} %copy.22), channel_id=1, source_target_pairs={{0,4},{4,8},{8,12},{12,16},{16,20},{20,24},{24,28},{28,32},{32,36}... | collective-permute-start | bytes 442376 | tf_op jit(solution)/shard_map/while/body/eval_jaxpr/ppermute | solution.py:14
  786.6 12.1 %collective-permute-start = (f32[32,1152]{1,0:T(8,128)S(1)}, f32[32,1152]{1,0:T(8,128)S(1)}, u32[]{:S(2)}, u32[]{:S(2)}) collective-permute-start(f32[32,1152]{1,0:T(8,128)S(1)} %copy.22), channel_id=1, source_target_pairs={{0,4},{4,8},{8,12},{12,16},{16,20},{20,24},{24,28},{28,32},{32,36}... | collective-permute-start | bytes 442376 | tf_op jit(solution)/shard_map/while/body/eval_jaxpr/ppermute | solution.py:14
  922.5 20.3 %all-to-all-start.2 = ((f32[64,3,288]{2,1,0:T(4,128)}), f32[64,3,288]{2,1,0:T(4,128)S(1)}, u32[]{:S(2)}, u32[]{:S(2)}) async-start(f32[64,3,288]{2,1,0:T(4,128)} %broadcast_select_fusion), calls=%async_computation.2 | async-start | bytes 786432 | tf_op jit(solution)/shard_map/all_to_all | solution.py:110
  (122 other events, 1253.9 us)
Sparse Core Ops, SparseCore 0:
  47.7 54.0 all-gather.2
  862.2 55.2 all-reduce.1
